TPU v7x, 256 devices: a whole 4x4x8 slice. The times are simulated.
256 devices in a mesh: row: 8 (over y, z_hi), col: 32 (over z_lo, x, core).
Axes of the slice: x: 4, y: 4, z: 8 (z_hi: 2, z_lo: 4; z = z_hi * 4 + z_lo), core: 2. Of those that a mesh axis runs over, the one named last changes fastest.
Arguments:
- transfer: bfloat16 [2, 4096, 16384], P(None, 'row', 'col'), may hold values from -0.046875 to 0.046875
- phase: float32 [16384, 128], P('col', 'row'), may hold values from -3.140625 to 3.140625
- trap_index: int32 [128, 64], replicated, may hold values from 0 to 4095
- levels: int32 [128, 64], replicated, may hold values from 1 to 4
- weights_old: float32 [128, 64], replicated, may hold values from 0.5 to 1.5
Outputs:
- far_field: bfloat16 [4096, 2, 128], P(('row', 'col'))
- weights_new: float32 [128, 64], replicated
- slm_field: float32 [16384, 2, 128], P('col', None, 'row')
All inputs are finite; a program needn't handle non-finite values.
Results may differ from a plain program's by a relative error of at most 0.013.
Values may be sent and summed in bfloat16 or wider, within the bound.
A program may use at most 64 MiB of HBM per device.

v0:
```python
import jax
import jax.numpy as jnp
from jax import lax
from jax.sharding import PartitionSpec as P

MODES = 16384
TRAPS = 64


def back_terms(transfer, piece):
    count = piece.shape[2]
    real_rows = transfer[0]
    imag_rows = transfer[1]
    stacked = jnp.concatenate([piece[:, 0], piece[:, 1]], axis=1)
    dims = (((0,), (0,)), ((), ()))
    first_b = lax.dot_general(real_rows, stacked, dims, preferred_element_type=jnp.float32)
    second_b = lax.dot_general(imag_rows, stacked, dims, preferred_element_type=jnp.float32)
    part = jnp.concatenate(
        [first_b[:, :count] + second_b[:, count:], first_b[:, count:] - second_b[:, :count]], axis=1
    )
    return part


def trap_lookup(block, trap_index, offset):
    count = block.shape[2]
    height = block.shape[0]
    local = trap_index - offset
    inside = (local >= 0) & (local < height)
    clipped = jnp.clip(local, 0, height - 1)
    pattern_ids = jnp.arange(count, dtype=jnp.int32)[:, None]
    values = block[clipped, :, pattern_ids]
    return (inside, clipped, pattern_ids, values)


def body(transfer, phase, trap_index, levels, weights_old):
    n_col = lax.axis_size("col")
    tile_rows = transfer.shape[1]
    pix_rows = tile_rows // n_col
    modes_local = transfer.shape[2]
    field = jnp.stack([jnp.cos(phase), jnp.sin(phase)], axis=0).astype(jnp.bfloat16)
    whole = lax.all_gather(field, "row", axis=2, tiled=True)
    count = whole.shape[2]
    joined = jnp.concatenate([whole[0], whole[1]], axis=1)
    target = levels.astype(jnp.float32)
    row_start = lax.axis_index("row") * tile_rows
    real_rows = transfer[0]
    imag_rows = transfer[1]
    first = jnp.dot(real_rows, joined, preferred_element_type=jnp.float32)
    second = jnp.dot(imag_rows, joined, preferred_element_type=jnp.float32)
    mine = lax.psum_scatter(
        jnp.stack(
            [first[:, :count] - second[:, count:], first[:, count:] + second[:, :count]], axis=1
        ),
        "col",
        scatter_dimension=0,
        tiled=True,
    )
    far_field = mine.astype(jnp.bfloat16)
    offset = row_start + lax.axis_index("col") * pix_rows
    inside, clipped, pattern_ids, values = trap_lookup(mine, trap_index, offset)
    amp_local = jnp.sqrt(values[..., 0] ** 2 + values[..., 1] ** 2 + 0.25)
    amp = lax.psum(jnp.where(inside, amp_local, 0.0), ("row", "col"))
    ratio = amp / target
    weights_new = weights_old * jnp.mean(ratio, axis=1, keepdims=True) / ratio
    coef = weights_new * target / amp
    adds = jnp.where(inside[..., None], coef[..., None] * values, 0.0)
    projected = (
        jnp.zeros(mine.shape, jnp.float32)
        .at[clipped, :, pattern_ids]
        .add(adds)
        .astype(jnp.bfloat16)
    )
    total = back_terms(transfer, lax.all_gather(projected, "col", axis=0, tiled=True))
    back = total.reshape(modes_local, 2, count)
    back = lax.psum_scatter(
        back.astype(jnp.bfloat16), "row", scatter_dimension=2, tiled=True
    ).astype(jnp.float32)
    scaled = jnp.sqrt(jnp.float32(MODES) / jnp.float32(TRAPS)) * back
    slm_field = scaled / jnp.sqrt(scaled[:, 0:1] ** 2 + scaled[:, 1:2] ** 2 + 1.0)
    return (far_field, weights_new, slm_field)


def solution(mesh):
    placed = (P(None, "row", "col"), P("col", "row"), P(), P(), P())
    return jax.shard_map(
        body,
        mesh=mesh,
        in_specs=placed,
        out_specs=(P(("row", "col"), None, None), P(), P("col", None, "row")),
        check_vma=False,
    )
```

profile of v0, /device:TPU:1, one launch (start us, length us, event | category | flops | bytes accessed | tf_op | source)
XLA Modules:
  0.0 715.4 jit_solution(8957432366630390848)
XLA Ops:
  7.2 0.9 fusion.20
  8.2 41.4 %all_gather.6 = bf16[2,512,128]{1,2,0:T(8,128)(2,1)S(1)} all-gather(bf16[2,512,16]{1,2,0:T(8,128)(2,1)S(1)} %pad_maximum_fusion.8), channel_id=1, replica_groups=mesh['row'=8,'col'=32] {'row'}, dimensions={2}, use_global_device_ids=true | all-gather | bytes 294912 | tf_op jit(solution)/shard_map/all_gather | solution.py:41
  49.6 1.4 convolution_bitcast_fusion.2
  50.9 1.4 convolution_bitcast_fusion.3
  52.3 0.1 fusion.13
  52.5 1.0 copy.31
  53.7 0.1 and_reduce_fusion
  53.8 0.1 copy.36
  54.0 0.1 copy.32
  54.1 0.6 dynamic-slice
  55.4 284.6 %all-reduce.3.cloned.1.call-done = f32[512,2,128]{2,1,0:T(2,128)} async-done(((f32[512,2,128]{2,1,0:T(2,128)}), f32[512,2,128]{2,1,0:T(2,128)}) %all-reduce.3.cloned.1.call-update) | async-done | bytes 524304
  340.0 1.3 fusion.27
  341.3 0.4 copy.33
  341.7 88.8 %gather_fusion = f32[8192,2]{1,0:T(8,128)} fusion(f32[16,2,128]{1,2,0:T(8,128)S(1)} %copy.33, s32[8192]{0:T(1024)S(1)} %reshape.27), kind=kCustom, calls=%fused_computation | custom fusion | bytes 196608 | tf_op jit(solution)/shard_map/gather | solution.py:31
  430.4 8.0 %fusion.28 = (f32[128,64,1]{2,1,0:T(8,128)}, f32[128,64,1]{2,1,0:T(8,128)}) fusion(f32[128,64,2]{2,1,0:T(8,128)} %bitcast.49), kind=kLoop, calls=%fused_computation.66 | loop fusion | bytes 131072 | tf_op jit(solution)/shard_map/slice | solution.py:61
  438.5 3.8 copy.40
  442.2 3.7 copy.41
  446.0 78.3 %psum.7 = f32[128,64]{0,1:T(8,128)S(1)} all-reduce(f32[128,64]{0,1:T(8,128)S(1)} %get-tuple-element.14), channel_id=1, replica_groups=mesh['row'=8,'col'=32] {'row','col'}, use_global_device_ids=true, to_apply=%region_1.2 | all-reduce | flops 8192 | bytes 65536 | tf_op jit(solution)/shard_map/psum | solution.py:62
  524.3 0.1 copy.37
  524.4 0.6 multiply_divide_fusion
  525.1 0.1 copy.38
  525.2 7.7 %multiply_select_fusion = f32[128,64,2]{2,1,0:T(8,128)} fusion(f32[128,64,2]{2,1,0:T(8,128)} %bitcast.50, f32[128,64]{1,0:T(8,128)S(1)} %copy.38, pred[128,64]{1,0:T(8,128)(4,1)S(1)} %copy.37), kind=kLoop, calls=%fused_computation.2 | loop fusion | flops 32768 | bytes 172032 | tf_op jit(solution)/shard_map/jit(_where)/select_n | solution.py:66
  532.9 56.5 %scatter_custom_fusion = f32[2048,2]{1,0:T(8,128)S(1)} fusion(s32[8192]{0:T(1024)S(1)} %reshape.33, f32[8192,2]{1,0:T(8,128)} %bitcast.51, f32[]{:T(128)} %constant.8.clone.1), kind=kCustom, calls=%fused_computation.12 | custom fusion | flops 16384 | bytes 16896
  589.5 0.2 copy.39
  589.7 39.2 %all_gather.7 = bf16[512,2,128]{2,0,1:T(8,128)(2,1)S(1)} all-gather(bf16[16,2,128]{2,0,1:T(8,128)(2,1)S(1)} %bitcast.54), channel_id=1, replica_groups=mesh['row'=8,'col'=32] {'col'}, dimensions={0}, use_global_device_ids=true | all-gather | bytes 270336 | tf_op jit(solution)/shard_map/all_gather | solution.py:73
  628.9 0.3 convolution_bitcast_fusion
  629.3 0.3 convolution_bitcast_fusion.1
  629.6 0.1 fusion.11
  629.7 0.7 pad_maximum_fusion.3
  630.4 75.9 %reduce-scatter.2.cloned.1.call-done = bf16[512,2,16]{0,2,1:T(8,128)(2,1)} async-done(((bf16[512,2,128]{0,2,1:T(8,128)(2,1)}), bf16[512,2,16]{0,2,1:T(8,128)(2,1)}) %reduce-scatter.2.cloned.1.call-update) | async-done | bytes 32784 | tf_op jit(solution)/shard_map/reduce_scatter | solution.py:75
  706.3 0.8 convert_multiply_fusion
  707.1 1.4 broadcast_divide_fusion
  (33 shorter events, 0.6 us)
Async XLA Ops:
  7.2 46.4 %copy-start.5 = (s32[2]{0:T(128)S(1)}, s32[2]{0:T(128)}, u32[]{:S(2)}) copy-start(s32[2]{0:T(128)} %constant.34) | copy-start | bytes 28
  7.2 46.5 %copy-start.4 = (s32[2]{0:T(128)S(1)}, s32[2]{0:T(128)}, u32[]{:S(2)}) copy-start(s32[2]{0:T(128)} %constant.37) | copy-start | bytes 28
  7.2 46.3 %copy-start.1 = (s32[128,64]{0,1:T(8,128)S(1)}, s32[128,64]{0,1:T(8,128)}, u32[]{:S(2)}) copy-start(s32[128,64]{0,1:T(8,128)} %param.7) | copy-start | bytes 98308
  7.2 332.8 %all-reduce.3.cloned.1.call-start = ((), (), s32[]{:S(2)}) async-start(), calls=%async_computation.2 | async-start | bytes 1048576
  8.1 46.0 %copy-start.6 = (u32[256]{0:T(256)S(1)}, u32[256]{0:T(256)}, u32[]{:S(2)}) copy-start(u32[256]{0:T(256)} %constant.57) | copy-start | bytes 3076
  53.5 652.8 %reduce-scatter.2.cloned.1.call-start = ((), (), s32[]{:S(2)}) async-start(), calls=%async_computation.1 | async-start | bytes 294912 | tf_op jit(solution)/shard_map/reduce_scatter | solution.py:75
  438.5 85.8 %copy-start.2 = (s32[128,64]{0,1:T(8,128)S(1)}, s32[128,64]{0,1:T(8,128)}, u32[]{:S(2)}) copy-start(s32[128,64]{0,1:T(8,128)} %param.8) | copy-start | bytes 98308
  438.5 86.0 %copy-start.3 = (f32[128,64]{0,1:T(8,128)S(1)}, f32[128,64]{0,1:T(8,128)}, u32[]{:S(2)}) copy-start(f32[128,64]{0,1:T(8,128)} %param.9) | copy-start | bytes 98308
  525.2 103.7 %copy-start = (bf16[2,512,512]{2,1,0:T(8,128)(2,1)S(1)}, bf16[2,512,512]{2,1,0:T(8,128)(2,1)}, u32[]{:S(2)}) copy-start(bf16[2,512,512]{2,1,0:T(8,128)(2,1)} %param.5) | copy-start | bytes 3145732
Sparse Core Ops, SparseCore 0:
  53.6 286.3 all-reduce.2
  630.6 75.7 reduce-scatter.1
where the time goes:
time: 717 us; the launch traced here: 715 us
  waiting for transfers between devices  361 us (50%)
  blocking collectives  159 us (22%)
  local copies, waits for them, and re-layouts  107 us (15%)
  other arithmetic  70.5 us (10%)
  between operations  14.9 us (2%)
    unnamed x3, waiting for transfers between devices  285 us
    gather x1, local copies, waits for them, and re-layouts, trap_lookup(): values = block[clipped, :, pattern_ids]  88.8 us
    psum x1, blocking collectives, body(): amp = lax.psum(jnp.where(inside, amp_local, 0.0), ('row', 'col'))  78.3 us
    reduce_scatter x1, waiting for transfers between devices, body(): lax.psum_scatter(back.astype(jnp.bfloat16), 'row', scatter_dimension=2, t...  75.9 us
    unnamed x4, other arithmetic  56.6 us
    all_gather x1, blocking collectives, body(): whole = lax.all_gather(field, 'row', axis=2, tiled=True)  41.4 us
    all_gather x1, blocking collectives, body(): lax.all_gather(projected, 'col', axis=0, tiled=True)  39.2 us
  transfers between devices with their start and end apart: 2, of which 2 were waited for; matrix products, arithmetic and copies ran while one was open for 0% of the time, Pallas kernels for 0%

commit v1 on v0

v1 whole, which is shorter than its diff:
```python
import functools

import jax
import jax.numpy as jnp
from jax import lax
from jax.experimental import pallas as pl
from jax.experimental.pallas import tpu as pltpu
from jax.sharding import PartitionSpec as P

MODES = 16384
TRAPS = 64
MESH = pl.DeviceIdType.MESH
CHUNKS = 4


def kernel(
    n_row,
    n_col,
    scale,
    transfer_hbm,
    phase_hbm,
    trap_hbm,
    levels_hbm,
    old_hbm,
    far_ref,
    weights_ref,
    slm_ref,
    transfer,
    phase,
    trap,
    levels,
    old,
    fields,
    part,
    rs_buf,
    out_all,
    power,
    amp_pix,
    stage,
    back_buf,
    amp_rows,
    amp_buf,
    in_sem,
    field_send,
    field_recv,
    rs_send,
    rs_recv,
    ag_send,
    ag_recv,
    back_send,
    back_recv,
    amp_send,
    amp_recv,
):
    row = lax.axis_index("row")
    col = lax.axis_index("col")
    pix_rows = part.shape[1]
    patterns = part.shape[2] // 2
    tile_rows = transfer.shape[1]
    own = phase.shape[0]
    traps = trap.shape[0]
    group = n_col // CHUNKS

    barrier = pltpu.get_barrier_semaphore()

    def greet_row(step, carry):
        peer = lax.rem(row + step, n_row)
        pl.semaphore_signal(barrier, inc=1, device_id=(peer, col), device_id_type=MESH)
        return carry

    def greet_col(step, carry):
        peer = lax.rem(col + step, n_col)
        pl.semaphore_signal(barrier, inc=1, device_id=(row, peer), device_id_type=MESH)
        return carry

    loads = [
        pltpu.make_async_copy(source, target, in_sem.at[index])
        for index, (source, target) in enumerate(
            (
                (phase_hbm, phase),
                (trap_hbm, trap),
                (levels_hbm, levels),
                (old_hbm, old),
                (transfer_hbm, transfer),
            )
        )
    ]
    for load in loads:
        load.start()
    lax.fori_loop(1, n_row, greet_row, 0)
    lax.fori_loop(1, n_col, greet_col, 0)

    loads[0].wait()
    angle = phase[...]
    fields[row, :own, :] = jnp.cos(angle).astype(jnp.bfloat16)
    fields[row, own:, :] = jnp.sin(angle).astype(jnp.bfloat16)

    for load in loads[1:4]:
        load.wait()
    row_start = row * tile_rows
    strip = min(tile_rows, 128)

    def power_strip(index, carry):
        base = pl.multiple_of(index * strip, strip)
        pixel = lax.broadcasted_iota(jnp.int32, (strip, patterns), 0) + (row_start + base)

        def add_trap(k, total):
            where = jnp.broadcast_to(trap[pl.ds(k, 1), :], (strip, patterns))
            target = levels[pl.ds(k, 1), :].astype(jnp.float32)
            value = old[pl.ds(k, 1), :] * target * target
            value = jnp.broadcast_to(value, (strip, patterns))
            return total + jnp.where(pixel == where, value, 0.0)

        power[pl.ds(base, strip), :] = lax.fori_loop(
            0, traps, add_trap, jnp.zeros((strip, patterns), jnp.float32)
        )
        return carry

    lax.fori_loop(0, tile_rows // strip, power_strip, 0)

    pl.semaphore_wait(barrier, n_row + n_col - 2)

    def field_copy(peer, slot, step):
        return pltpu.make_async_remote_copy(
            src_ref=fields.at[slot],
            dst_ref=fields.at[slot],
            send_sem=field_send.at[step],
            recv_sem=field_recv.at[slot],
            device_id=(peer, col),
            device_id_type=MESH,
        )

    def send_field(step, carry):
        field_copy(lax.rem(row + step, n_row), row, step).start()
        return carry

    def take_field(step, carry):
        peer = lax.rem(row + n_row - step, n_row)
        field_copy(peer, peer, step).wait_recv()
        return carry

    lax.fori_loop(1, n_row, send_field, 0)
    loads[4].wait()
    lax.fori_loop(1, n_row, take_field, 0)

    field_re = fields[:, :own, :].reshape(patterns, phase.shape[1])
    field_im = fields[:, own:, :].reshape(patterns, phase.shape[1])
    with_real = jnp.concatenate([field_re, field_im], axis=0)
    with_imag = jnp.concatenate([-field_im, field_re], axis=0)
    over_modes = (((1,), (1,)), ((), ()))

    def rs_copy(peer, source, slot, step):
        return pltpu.make_async_remote_copy(
            src_ref=part.at[source],
            dst_ref=rs_buf.at[slot],
            send_sem=rs_send.at[step],
            recv_sem=rs_recv.at[slot],
            device_id=(row, peer),
            device_id_type=MESH,
        )

    my_chunk = col // group
    rows_per = group * pix_rows
    for turn in range(CHUNKS):
        chunk = lax.rem(my_chunk + turn + 1, CHUNKS)
        base = pl.multiple_of(chunk * rows_per, rows_per)
        first = lax.dot_general(
            transfer[0, pl.ds(base, rows_per), :], with_real, over_modes, preferred_element_type=jnp.float32
        )
        second = lax.dot_general(
            transfer[1, pl.ds(base, rows_per), :], with_imag, over_modes, preferred_element_type=jnp.float32
        )
        part[pl.ds(chunk * group, group)] = (
            (first + second).astype(jnp.bfloat16).reshape(group, pix_rows, 2 * patterns)
        )

        def send_part(index, carry):
            peer = chunk * group + lax.rem(index + col, group)

            @pl.when(peer != col)
            def _():
                rs_copy(peer, peer, col, peer).start()

            return carry

        lax.fori_loop(0, group, send_part, 0)

    def add_part(step, total):
        peer = lax.rem(col + n_col - step, n_col)
        rs_copy(peer, peer, peer, step).wait_recv()
        return total + rs_buf[peer].astype(jnp.float32)

    mine = lax.fori_loop(1, n_col, add_part, part[col].astype(jnp.float32)).astype(jnp.bfloat16)
    far_ref[...] = mine
    out_all[col] = mine

    def ag_copy(peer, slot, step):
        return pltpu.make_async_remote_copy(
            src_ref=out_all.at[slot],
            dst_ref=out_all.at[slot],
            send_sem=ag_send.at[step],
            recv_sem=ag_recv.at[slot],
            device_id=(row, peer),
            device_id_type=MESH,
        )

    def send_out(step, carry):
        ag_copy(lax.rem(col + step, n_col), col, step).start()
        return carry

    def take_out(step, carry):
        peer = lax.rem(col + n_col - step, n_col)
        ag_copy(peer, peer, step).wait_recv()
        return carry

    lax.fori_loop(1, n_col, send_out, 0)
    lax.fori_loop(1, n_col, take_out, 0)

    whole = out_all[...].reshape(tile_rows, 2 * patterns)
    out_re = whole[:, :patterns].astype(jnp.float32)
    out_im = whole[:, patterns:].astype(jnp.float32)
    square = out_re * out_re + out_im * out_im + 0.25
    amp_pix[...] = jnp.sqrt(square)
    gain = power[...] / square
    proj_re = (gain * out_re).astype(jnp.bfloat16).T
    proj_im = (gain * out_im).astype(jnp.bfloat16).T
    left_real = jnp.concatenate([proj_re, proj_im], axis=0)
    left_imag = jnp.concatenate([proj_im, -proj_re], axis=0)
    back = jnp.dot(left_real, transfer[0], preferred_element_type=jnp.float32) + jnp.dot(
        left_imag, transfer[1], preferred_element_type=jnp.float32
    )
    back = back.astype(jnp.bfloat16)
    stage[:, :own, :] = back[:patterns].reshape(n_row, own, back.shape[1])
    stage[:, own:, :] = back[patterns:].reshape(n_row, own, back.shape[1])

    def back_copy(peer, source, slot, step):
        return pltpu.make_async_remote_copy(
            src_ref=stage.at[source],
            dst_ref=back_buf.at[slot],
            send_sem=back_send.at[step],
            recv_sem=back_recv.at[slot],
            device_id=(peer, col),
            device_id_type=MESH,
        )

    def send_back(step, carry):
        peer = lax.rem(row + step, n_row)
        back_copy(peer, peer, row, step).start()
        return carry

    lax.fori_loop(1, n_row, send_back, 0)

    def find_trap(k, carry):
        where = jnp.broadcast_to(trap[pl.ds(k, 1), :], (tile_rows, patterns)) - row_start
        pixel = lax.broadcasted_iota(jnp.int32, (tile_rows, patterns), 0)
        found = jnp.where(pixel == where, amp_pix[...], 0.0)
        amp_rows[pl.ds(k, 1), :] = jnp.sum(found, axis=0, keepdims=True)
        return carry

    lax.fori_loop(0, traps, find_trap, 0)
    amp_buf[row] = amp_rows[...].astype(jnp.bfloat16)

    def amp_copy(peer, slot, step):
        return pltpu.make_async_remote_copy(
            src_ref=amp_buf.at[slot],
            dst_ref=amp_buf.at[slot],
            send_sem=amp_send.at[step],
            recv_sem=amp_recv.at[slot],
            device_id=(peer, col),
            device_id_type=MESH,
        )

    def send_amp(step, carry):
        amp_copy(lax.rem(row + step, n_row), row, step).start()
        return carry

    def add_back(step, total):
        peer = lax.rem(row + n_row - step, n_row)
        back_copy(peer, peer, peer, step).wait_recv()
        return total + back_buf[peer].astype(jnp.float32)

    def take_amp(step, carry):
        peer = lax.rem(row + n_row - step, n_row)
        amp_copy(peer, peer, step).wait_recv()
        return carry

    lax.fori_loop(1, n_row, send_amp, 0)
    total = lax.fori_loop(1, n_row, add_back, stage[row].astype(jnp.float32))
    lax.fori_loop(1, n_row, take_amp, 0)

    amp = jnp.sum(amp_buf[...].astype(jnp.float32), axis=0)
    ratio = amp / levels[...].astype(jnp.float32)
    mean = jnp.mean(ratio, axis=0, keepdims=True)
    weights_ref[...] = old[...] * mean / ratio
    lane = lax.broadcasted_iota(jnp.int32, (own, patterns), 1)
    place = lax.broadcasted_iota(jnp.int32, (own, patterns), 0) + row * own
    mine_mean = jnp.sum(
        jnp.where(lane == place, jnp.broadcast_to(mean, (own, patterns)), 0.0), axis=1, keepdims=True
    )
    factor = scale * mine_mean
    scaled_re = factor * total[:own]
    scaled_im = factor * total[own:]
    norm = jnp.sqrt(scaled_re * scaled_re + scaled_im * scaled_im + 1.0)
    slm_ref[0] = scaled_re / norm
    slm_ref[1] = scaled_im / norm

    def drain_row(step, carry):
        peer = lax.rem(row + step, n_row)
        field_copy(peer, row, step).wait_send()
        back_copy(peer, peer, row, step).wait_send()
        amp_copy(peer, row, step).wait_send()
        return carry

    def drain_col(step, carry):
        peer = lax.rem(col + step, n_col)
        rs_copy(peer, peer, col, peer).wait_send()
        ag_copy(peer, col, step).wait_send()
        return carry

    lax.fori_loop(1, n_row, drain_row, 0)
    lax.fori_loop(1, n_col, drain_col, 0)


def body(transfer, phase, trap_index, levels, weights_old):
    n_row = lax.axis_size("row")
    n_col = lax.axis_size("col")
    patterns, traps = trap_index.shape
    tile_rows, modes = transfer.shape[1:]
    pix_rows = tile_rows // n_col
    own = phase.shape[1]
    f32, bf16, i32 = jnp.float32, jnp.bfloat16, jnp.int32
    dma = pltpu.SemaphoreType.DMA
    far, weights, slm = pl.pallas_call(
        functools.partial(kernel, n_row, n_col, (MODES / TRAPS) ** 0.5),
        out_shape=(
            jax.ShapeDtypeStruct((pix_rows, 2 * patterns), bf16),
            jax.ShapeDtypeStruct((traps, patterns), f32),
            jax.ShapeDtypeStruct((2, own, modes), f32),
        ),
        in_specs=[pl.BlockSpec(memory_space=pl.ANY)] * 5,
        out_specs=[pl.BlockSpec(memory_space=pltpu.VMEM)] * 3,
        scratch_shapes=[
            pltpu.VMEM(transfer.shape, bf16),
            pltpu.VMEM((own, modes), f32),
            pltpu.VMEM((traps, patterns), i32),
            pltpu.VMEM((traps, patterns), i32),
            pltpu.VMEM((traps, patterns), f32),
            pltpu.VMEM((n_row, 2 * own, modes), bf16),
            pltpu.VMEM((n_col, pix_rows, 2 * patterns), bf16),
            pltpu.VMEM((n_col, pix_rows, 2 * patterns), bf16),
            pltpu.VMEM((n_col, pix_rows, 2 * patterns), bf16),
            pltpu.VMEM((tile_rows, patterns), f32),
            pltpu.VMEM((tile_rows, patterns), f32),
            pltpu.VMEM((n_row, 2 * own, modes), bf16),
            pltpu.VMEM((n_row, 2 * own, modes), bf16),
            pltpu.VMEM((traps, patterns), f32),
            pltpu.VMEM((n_row, traps, patterns), bf16),
            dma((5,)),
        ]
        + [dma((count,)) for count in (n_row, n_row, n_col, n_col, n_col, n_col, n_row, n_row, n_row, n_row)],
        compiler_params=pltpu.CompilerParams(
            collective_id=0, has_side_effects=True, vmem_limit_bytes=48 * 1024 * 1024
        ),
    )(transfer, phase.T, trap_index.T, levels.T, weights_old.T)
    return (far.reshape(pix_rows, 2, patterns), weights.T, slm.transpose(2, 0, 1))


def solution(mesh):
    placed = (P(None, "row", "col"), P("col", "row"), P(), P(), P())
    return jax.shard_map(
        body,
        mesh=mesh,
        in_specs=placed,
        out_specs=(P(("row", "col"), None, None), P(), P("col", None, "row")),
        check_vma=False,
    )
```

time: 717 us -> 57.7 us (0.08)
  waiting for transfers between devices: 361 us -> 0 us
  blocking collectives: 159 us -> 0 us
  local copies, waits for them, and re-layouts: 107 us -> 6.1 us
  other arithmetic: 70.5 us -> 0 us
  Pallas kernels: 0 us -> 50.6 us
  between operations: 14.9 us -> 0.65 us
    unnamed x3 -> x0, waiting for transfers between devices: 285 us -> none
    gather x1 -> x0, local copies, waits for them, and re-layouts: 88.8 us -> none  [trap_lookup(): values = block[clipped, :, pattern_ids]]
    all_gather x2 -> x0, blocking collectives: 80.6 us -> none  [the longest x1 41.4 us: body(): whole = lax.all_gather(field, 'row', axis=2, tiled=True)]
    psum x1 -> x0, blocking collectives: 78.3 us -> none  [body(): amp = lax.psum(jnp.where(inside, amp_local, 0.0), ('row', 'col'))]
    reduce_scatter x1 -> x0, waiting for transfers between devices: 75.9 us -> none  [body(): lax.psum_scatter(back.astype(jnp.bfloat16), 'row', scatter_dimension=2, t...]
    unnamed x4 -> x0, other arithmetic: 56.6 us -> none
    pallas_call x0 -> x1, Pallas kernels: none -> 50.6 us  [body(): pl.pallas_call(functools.partial(kernel, n_row, n_col, (MODES / TRAPS) **...]
    slice x1 -> x0, local copies, waits for them, and re-layouts: 8.03 us -> none  [body(): amp_local = jnp.sqrt(values[..., 0] ** 2 + values[..., 1] ** 2 + 0.25)]
  transfers between devices with their start and end apart: 2 -> 0, of which waited for: 2 -> 0; matrix products, arithmetic and copies ran while one was open for 0% -> 0% of each run, Pallas kernels for 0% -> 0%
where the time goes in v1:
time: 57.7 us; the launch traced here: 57.3 us
  Pallas kernels  50.6 us (88%)
  local copies, waits for them, and re-layouts  6.1 us (11%)
  between operations  0.65 us (1%)
    pallas_call x1, Pallas kernels, body(): pl.pallas_call(functools.partial(kernel, n_row, n_col, (MODES / TRAPS) **...  50.6 us
    unnamed x12, local copies, waits for them, and re-layouts  5.49 us

profile of v1, /device:TPU:1, one launch (start us, length us, event | category | flops | bytes accessed | tf_op | source)
XLA Modules:
  0.0 57.3 jit_solution(10818653197966219689)
XLA Ops:
  0.6 0.0 copy-start
  0.6 1.2 %copy-done = bf16[2,512,512]{2,1,0:T(8,128)(2,1)S(1)} copy-done((bf16[2,512,512]{2,1,0:T(8,128)(2,1)S(1)}, bf16[2,512,512]{2,1,0:T(8,128)(2,1)}, u32[]{:S(2)}) %copy-start) | copy-done | bytes 1048600
  1.9 0.0 copy-start.1
  1.9 0.8 %copy-done.1 = f32[512,16]{0,1:T(8,128)S(1)} copy-done((f32[512,16]{0,1:T(8,128)S(1)}, f32[512,16]{0,1:T(8,128)}, u32[]{:S(2)}) %copy-start.1) | copy-done | bytes 32792
  2.6 0.0 copy-start.2
  2.6 0.8 %copy-done.2 = s32[128,64]{0,1:T(8,128)S(1)} copy-done((s32[128,64]{0,1:T(8,128)S(1)}, s32[128,64]{0,1:T(8,128)}, u32[]{:S(2)}) %copy-start.2) | copy-done | bytes 32792
  3.4 0.0 copy-start.3
  3.4 0.8 %copy-done.3 = s32[128,64]{0,1:T(8,128)S(1)} copy-done((s32[128,64]{0,1:T(8,128)S(1)}, s32[128,64]{0,1:T(8,128)}, u32[]{:S(2)}) %copy-start.3) | copy-done | bytes 32792
  4.1 0.0 copy-start.4
  4.1 0.8 %copy-done.4 = f32[128,64]{0,1:T(8,128)S(1)} copy-done((f32[128,64]{0,1:T(8,128)S(1)}, f32[128,64]{0,1:T(8,128)}, u32[]{:S(2)}) %copy-start.4) | copy-done | bytes 32792
  4.9 50.6 %shard_map.76 = (bf16[16,256]{1,0:T(8,128)(2,1)S(1)}, f32[64,128]{1,0:T(8,128)S(1)}, f32[2,16,512]{2,1,0:T(8,128)S(1)}) custom-call(bf16[2,512,512]{2,1,0:T(8,128)(2,1)S(1)} %copy-done, f32[16,512]{1,0:T(8,128)S(1)} %bitcast.7, s32[64,128]{1,0:T(8,128)S(1)} %bitcast.8, s32[64,128]{1,0:T(8,128)S(1)} %bitcast.9, f32[64,128]{1,0:T(8,128)S(1)} %bitcast.10), custom_call_target="tpu_custom_call" | custom-call | tf_op jit(solution)/shard_map/pallas_call | solution.py:333
  55.5 0.6 %reshape.9 = bf16[16,2,128]{2,1,0:T(2,128)(2,1)} reshape(bf16[16,256]{1,0:T(8,128)(2,1)S(1)} %get-tuple-element.6) | data formatting | bytes 16384 | tf_op jit(solution)/shard_map/reshape | solution.py:365
  56.1 0.6 %copy.10 = f32[128,64]{0,1:T(8,128)} copy(f32[128,64]{0,1:T(8,128)S(1)} %bitcast.11) | data formatting | bytes 65536
  56.7 0.6 %copy.11 = f32[512,2,16]{0,2,1:T(8,128)} copy(f32[512,2,16]{0,2,1:T(8,128)S(1)} %bitcast.6) | data formatting | bytes 131072
Async XLA Ops:
  0.6 1.2 %copy-start = (bf16[2,512,512]{2,1,0:T(8,128)(2,1)S(1)}, bf16[2,512,512]{2,1,0:T(8,128)(2,1)}, u32[]{:S(2)}) copy-start(bf16[2,512,512]{2,1,0:T(8,128)(2,1)} %transfer_hbm.1) | copy-start | bytes 3145732
  1.9 0.8 %copy-start.1 = (f32[512,16]{0,1:T(8,128)S(1)}, f32[512,16]{0,1:T(8,128)}, u32[]{:S(2)}) copy-start(f32[512,16]{0,1:T(8,128)} %param.6) | copy-start | bytes 98308
  2.6 0.8 %copy-start.2 = (s32[128,64]{0,1:T(8,128)S(1)}, s32[128,64]{0,1:T(8,128)}, u32[]{:S(2)}) copy-start(s32[128,64]{0,1:T(8,128)} %param.7) | copy-start | bytes 98308
  3.4 0.8 %copy-start.3 = (s32[128,64]{0,1:T(8,128)S(1)}, s32[128,64]{0,1:T(8,128)}, u32[]{:S(2)}) copy-start(s32[128,64]{0,1:T(8,128)} %param.8) | copy-start | bytes 98308
  4.1 0.8 %copy-start.4 = (f32[128,64]{0,1:T(8,128)S(1)}, f32[128,64]{0,1:T(8,128)}, u32[]{:S(2)}) copy-start(f32[128,64]{0,1:T(8,128)} %param.9) | copy-start | bytes 98308

commit v2 on v1

v2 whole, which is shorter than its diff:
```python
import functools

import jax
import jax.numpy as jnp
from jax import lax
from jax.experimental import pallas as pl
from jax.experimental.pallas import tpu as pltpu
from jax.sharding import PartitionSpec as P

MODES = 16384
TRAPS = 64
MESH = pl.DeviceIdType.MESH
CHUNKS = 4


def kernel(
    n_row,
    n_col,
    scale,
    transfer_hbm,
    phase_hbm,
    trap_hbm,
    levels_hbm,
    old_hbm,
    far_ref,
    weights_ref,
    slm_ref,
    transfer,
    phase,
    trap,
    levels,
    old,
    fields,
    kept,
    pair_out,
    pair_in,
    part,
    rs_buf,
    out_all,
    power,
    amp_pix,
    stage,
    back_buf,
    half_out,
    half_in,
    amp_rows,
    amp_buf,
    amp_out,
    amp_in,
    in_sem,
    field_send,
    field_recv,
    pair_send,
    pair_recv,
    rs_send,
    rs_recv,
    ag_send,
    ag_recv,
    share_send,
    back_send,
    back_recv,
    amp_send,
    amp_recv,
    half_send,
    half_recv,
):
    row = lax.axis_index("row")
    col = lax.axis_index("col")
    core = lax.rem(col, 2)
    chip = col // 2
    n_chip = n_col // 2
    n_y = n_row // 2
    mate = col + 1 - 2 * core
    across = row + 1 - 2 * lax.rem(row, 2)
    pix_rows, patterns = rs_buf.shape[1], rs_buf.shape[2] // 2
    tile_rows = transfer.shape[1]
    own, modes = phase.shape
    traps = trap.shape[0]
    group = n_col // CHUNKS
    half = group // 2
    rows_per = group * pix_rows

    def along_y(step):
        return lax.rem(row + 2 * step, n_row)

    def before_y(step):
        return lax.rem(row + n_row - 2 * step, n_row)

    def chip_col(step):
        return 2 * lax.rem(chip + step, n_chip) + core

    def chip_before(step):
        return 2 * lax.rem(chip + n_chip - step, n_chip) + core

    def greet(device):
        pl.semaphore_signal(barrier, inc=1, device_id=device, device_id_type=MESH)

    barrier = pltpu.get_barrier_semaphore()
    greet((across, col))

    def greet_y(step, carry):
        greet((along_y(step), col))
        return carry

    def greet_chip(step, carry):
        greet((row, chip_col(step)))
        return carry

    lax.fori_loop(1, n_y, greet_y, 0)
    lax.fori_loop(1, n_chip, greet_chip, 0)
    greet((row, mate))

    loads = [
        pltpu.make_async_copy(source, target, in_sem.at[index])
        for index, (source, target) in enumerate(
            (
                (phase_hbm, phase),
                (trap_hbm, trap),
                (levels_hbm, levels),
                (old_hbm, old),
                (transfer_hbm, transfer),
            )
        )
    ]
    for load in loads:
        load.start()

    loads[0].wait()
    angle = phase[...]
    fields[row, :own, :] = jnp.cos(angle).astype(jnp.bfloat16)
    fields[row, own:, :] = jnp.sin(angle).astype(jnp.bfloat16)

    for load in loads[1:4]:
        load.wait()
    row_start = row * tile_rows
    strip = min(tile_rows, 128)

    def power_strip(index, carry):
        base = pl.multiple_of(index * strip, strip)
        pixel = lax.broadcasted_iota(jnp.int32, (strip, patterns), 0) + (row_start + base)

        def add_trap(k, total):
            where = jnp.broadcast_to(trap[pl.ds(k, 1), :], (strip, patterns))
            target = levels[pl.ds(k, 1), :].astype(jnp.float32)
            value = old[pl.ds(k, 1), :] * target * target
            value = jnp.broadcast_to(value, (strip, patterns))
            return total + jnp.where(pixel == where, value, 0.0)

        power[pl.ds(base, strip), :] = lax.fori_loop(
            0, traps, add_trap, jnp.zeros((strip, patterns), jnp.float32)
        )
        return carry

    lax.fori_loop(0, tile_rows // strip, power_strip, 0)
    pl.semaphore_wait(barrier, n_y + n_chip)

    def field_copy(peer, slot, step):
        return pltpu.make_async_remote_copy(
            src_ref=fields.at[slot],
            dst_ref=fields.at[slot],
            send_sem=field_send.at[step],
            recv_sem=field_recv.at[slot],
            device_id=(peer, col),
            device_id_type=MESH,
        )

    field_copy(across, row, 0).start()

    def send_own(step, carry):
        field_copy(along_y(step), row, step).start()
        return carry

    def send_across(step, carry):
        field_copy(along_y(step), across, n_y + step).start()
        return carry

    def take_field(step, carry):
        peer = before_y(step)
        field_copy(row, peer, step).wait_recv()
        return carry

    def take_across(step, carry):
        peer = lax.rem(across + n_row - 2 * step, n_row)
        field_copy(row, peer, step).wait_recv()
        return carry

    lax.fori_loop(1, n_y, send_own, 0)
    loads[4].wait()
    field_copy(across, across, 0).wait_recv()
    lax.fori_loop(1, n_y, send_across, 0)
    lax.fori_loop(1, n_y, take_field, 0)
    lax.fori_loop(1, n_y, take_across, 0)

    field_re = fields[:, :own, :].reshape(patterns, modes)
    field_im = fields[:, own:, :].reshape(patterns, modes)
    with_real = jnp.concatenate([field_re, field_im], axis=0)
    with_imag = jnp.concatenate([-field_im, field_re], axis=0)
    over_modes = (((1,), (1,)), ((), ()))

    def pair_copy(chunk):
        return pltpu.make_async_remote_copy(
            src_ref=pair_out.at[chunk],
            dst_ref=pair_in.at[chunk],
            send_sem=pair_send.at[chunk],
            recv_sem=pair_recv.at[chunk],
            device_id=(row, mate),
            device_id_type=MESH,
        )

    def rs_copy(peer, source, slot, step):
        return pltpu.make_async_remote_copy(
            src_ref=part.at[source],
            dst_ref=rs_buf.at[slot],
            send_sem=rs_send.at[step],
            recv_sem=rs_recv.at[slot],
            device_id=(row, peer),
            device_id_type=MESH,
        )

    my_chunk = col // group

    def order(turn):
        return lax.rem(my_chunk + turn + 1, CHUNKS)

    def make_chunk(chunk):
        base = pl.multiple_of(chunk * rows_per, rows_per)
        both = lax.dot_general(
            transfer[0, pl.ds(base, rows_per), :], with_real, over_modes, preferred_element_type=jnp.float32
        ) + lax.dot_general(
            transfer[1, pl.ds(base, rows_per), :], with_imag, over_modes, preferred_element_type=jnp.float32
        )
        both = both.reshape(half, 2, pix_rows, 2 * patterns)
        first = core == 0
        kept[chunk] = jnp.where(first, both[:, 0], both[:, 1])
        pair_out[chunk] = jnp.where(first, both[:, 1], both[:, 0]).astype(jnp.bfloat16)
        pair_copy(chunk).start()

    def send_chunk(chunk):
        pair_copy(chunk).wait_recv()
        total = kept[chunk] + pair_in[chunk].astype(jnp.float32)
        part[pl.ds(chunk * half, half)] = total.astype(jnp.bfloat16)

        def send_part(index, carry):
            target = chunk * half + lax.rem(index + chip, half)

            @pl.when(target != chip)
            def _():
                rs_copy(2 * target + core, target, chip, target).start()

            return carry

        lax.fori_loop(0, half, send_part, 0)

    make_chunk(order(0))
    for turn in range(1, CHUNKS):
        make_chunk(order(turn))
        send_chunk(order(turn - 1))
    send_chunk(order(CHUNKS - 1))

    def add_part(step, total):
        source = lax.rem(chip + n_chip - step, n_chip)
        rs_copy(col, source, source, 0).wait_recv()
        return total + rs_buf[source].astype(jnp.float32)

    mine = lax.fori_loop(1, n_chip, add_part, part[chip].astype(jnp.float32)).astype(jnp.bfloat16)
    far_ref[...] = mine
    out_all[col] = mine

    def ag_copy(peer, slot, step):
        return pltpu.make_async_remote_copy(
            src_ref=out_all.at[slot],
            dst_ref=out_all.at[slot],
            send_sem=ag_send.at[step],
            recv_sem=ag_recv.at[slot],
            device_id=(row, peer),
            device_id_type=MESH,
        )

    def share_copy(slot, step):
        return pltpu.make_async_remote_copy(
            src_ref=out_all.at[slot],
            dst_ref=out_all.at[slot],
            send_sem=share_send.at[step],
            recv_sem=ag_recv.at[slot],
            device_id=(row, mate),
            device_id_type=MESH,
        )

    def send_out(step, carry):
        ag_copy(chip_col(step), col, step).start()
        return carry

    def share_out(step, carry):
        slot = chip_before(step)
        ag_copy(col, slot, step).wait_recv()
        share_copy(slot, step).start()
        return carry

    def take_shared(step, carry):
        slot = chip_before(step) + 1 - 2 * core
        share_copy(slot, step).wait_recv()
        return carry

    lax.fori_loop(1, n_chip, send_out, 0)
    share_copy(col, 0).start()
    lax.fori_loop(1, n_chip, share_out, 0)
    lax.fori_loop(0, n_chip, take_shared, 0)

    whole = out_all[...].reshape(tile_rows, 2 * patterns)
    out_re = whole[:, :patterns].astype(jnp.float32)
    out_im = whole[:, patterns:].astype(jnp.float32)
    square = out_re * out_re + out_im * out_im + 0.25
    amp_pix[...] = jnp.sqrt(square).reshape(amp_pix.shape)
    gain = power[...] / square
    proj_re = (gain * out_re).astype(jnp.bfloat16).T
    proj_im = (gain * out_im).astype(jnp.bfloat16).T
    left_real = jnp.concatenate([proj_re, proj_im], axis=0)
    left_imag = jnp.concatenate([proj_im, -proj_re], axis=0)
    back = jnp.dot(left_real, transfer[0], preferred_element_type=jnp.float32) + jnp.dot(
        left_imag, transfer[1], preferred_element_type=jnp.float32
    )
    back = back.astype(jnp.bfloat16)
    stage[:, :own, :] = back[:patterns].reshape(n_row, own, modes)
    stage[:, own:, :] = back[patterns:].reshape(n_row, own, modes)

    def back_copy(peer, source, slot):
        return pltpu.make_async_remote_copy(
            src_ref=stage.at[source],
            dst_ref=back_buf.at[slot],
            send_sem=back_send.at[slot],
            recv_sem=back_recv.at[slot],
            device_id=(peer, col),
            device_id_type=MESH,
        )

    def send_far(step, carry):
        back_copy(along_y(step), lax.rem(across + 2 * step, n_row), n_y + step).start()
        return carry

    def send_near(step, carry):
        back_copy(along_y(step), along_y(step), step).start()
        return carry

    lax.fori_loop(1, n_y, send_far, 0)
    lax.fori_loop(1, n_y, send_near, 0)

    lanes = 8
    tiles = tile_rows // lanes

    def find_trap(k, carry):
        local = jnp.broadcast_to(trap[pl.ds(k, 1), :], (lanes, patterns)) - row_start
        width = tiles // 2
        upper = (local & (width * lanes)) != 0
        chosen = jnp.where(upper[None], amp_pix[pl.ds(width, width)], amp_pix[pl.ds(0, width)])
        while width > 1:
            width //= 2
            upper = (local & (width * lanes)) != 0
            chosen = jnp.where(upper[None], chosen[width:], chosen[:width])
        sub = lax.broadcasted_iota(jnp.int32, (lanes, patterns), 0)
        hit = ((local & (lanes - 1)) == sub) & (local >= 0) & (local < tile_rows)
        amp_rows[pl.ds(k, 1), :] = jnp.sum(jnp.where(hit, chosen[0], 0.0), axis=0, keepdims=True)
        return carry

    lax.fori_loop(0, traps, find_trap, 0, unroll=2)
    amp_out[0] = amp_rows[...].astype(jnp.bfloat16)

    def amp_copy(peer, slot):
        return pltpu.make_async_remote_copy(
            src_ref=amp_out.at[0],
            dst_ref=amp_buf.at[slot],
            send_sem=amp_send.at[slot],
            recv_sem=amp_recv.at[slot],
            device_id=(peer, col),
            device_id_type=MESH,
        )

    def send_amp(step, carry):
        amp_copy(along_y(step), step).start()
        return carry

    def add_far(step, total):
        back_copy(row, row, n_y + step).wait_recv()
        return total + back_buf[n_y + step].astype(jnp.float32)

    def add_near(step, total):
        back_copy(row, row, step).wait_recv()
        return total + back_buf[step].astype(jnp.float32)

    def add_amp(step, total):
        amp_copy(row, step).wait_recv()
        return total + amp_buf[step].astype(jnp.float32)

    lax.fori_loop(1, n_y, send_amp, 0)
    half_out[...] = lax.fori_loop(1, n_y, add_far, stage[across].astype(jnp.float32)).astype(jnp.bfloat16)
    half_copy = pltpu.make_async_remote_copy(
        src_ref=half_out,
        dst_ref=half_in,
        send_sem=half_send.at[0],
        recv_sem=half_recv.at[0],
        device_id=(across, col),
        device_id_type=MESH,
    )
    half_copy.start()
    amp_half = lax.fori_loop(1, n_y, add_amp, amp_out[0].astype(jnp.float32))
    amp_out[1] = amp_half.astype(jnp.bfloat16)
    amp_across = pltpu.make_async_remote_copy(
        src_ref=amp_out.at[1],
        dst_ref=amp_in,
        send_sem=half_send.at[1],
        recv_sem=half_recv.at[1],
        device_id=(across, col),
        device_id_type=MESH,
    )
    amp_across.start()
    near = lax.fori_loop(1, n_y, add_near, stage[row].astype(jnp.float32))
    half_copy.wait_recv()
    total = near + half_in[...].astype(jnp.float32)
    amp_across.wait_recv()

    amp = amp_half + amp_in[...].astype(jnp.float32)
    ratio = amp / levels[...].astype(jnp.float32)
    mean = jnp.mean(ratio, axis=0, keepdims=True)
    weights_ref[...] = old[...] * mean / ratio
    lane = lax.broadcasted_iota(jnp.int32, (own, patterns), 1)
    place = lax.broadcasted_iota(jnp.int32, (own, patterns), 0) + row * own
    mine_mean = jnp.sum(
        jnp.where(lane == place, jnp.broadcast_to(mean, (own, patterns)), 0.0), axis=1, keepdims=True
    )
    factor = scale * mine_mean
    scaled_re = factor * total[:own]
    scaled_im = factor * total[own:]
    norm = jnp.sqrt(scaled_re * scaled_re + scaled_im * scaled_im + 1.0)
    slm_ref[0] = scaled_re / norm
    slm_ref[1] = scaled_im / norm

    def drain_y(step, carry):
        field_copy(row, row, step).wait_send()
        field_copy(row, row, n_y + step).wait_send()
        back_copy(row, row, step).wait_send()
        back_copy(row, row, n_y + step).wait_send()
        amp_copy(row, step).wait_send()
        return carry

    def drain_chip(step, carry):
        target = lax.rem(chip + step, n_chip)
        rs_copy(col, target, chip, target).wait_send()
        ag_copy(col, col, step).wait_send()
        share_copy(col, step).wait_send()
        return carry

    field_copy(across, row, 0).wait_send()
    share_copy(col, 0).wait_send()
    for chunk in range(CHUNKS):
        pair_copy(chunk).wait_send()
    lax.fori_loop(1, n_y, drain_y, 0)
    lax.fori_loop(1, n_chip, drain_chip, 0)
    half_copy.wait_send()
    amp_across.wait_send()


def body(transfer, phase, trap_index, levels, weights_old):
    n_row = lax.axis_size("row")
    n_col = lax.axis_size("col")
    patterns, traps = trap_index.shape
    tile_rows, modes = transfer.shape[1:]
    pix_rows = tile_rows // n_col
    own = phase.shape[1]
    n_y, n_chip = n_row // 2, n_col // 2
    half = n_chip // CHUNKS
    f32, bf16, i32 = jnp.float32, jnp.bfloat16, jnp.int32
    dma = pltpu.SemaphoreType.DMA
    arrays = (transfer, phase.T, trap_index.T, levels.T, weights_old.T)
    block = (pix_rows, 2 * patterns)
    far, weights, slm = pl.pallas_call(
        functools.partial(kernel, n_row, n_col, (MODES / TRAPS) ** 0.5),
        out_shape=(
            jax.ShapeDtypeStruct(block, bf16),
            jax.ShapeDtypeStruct((traps, patterns), f32),
            jax.ShapeDtypeStruct((2, own, modes), f32),
        ),
        in_specs=[pl.BlockSpec(memory_space=pl.ANY)] * 5,
        out_specs=[pl.BlockSpec(memory_space=pltpu.VMEM)] * 3,
        scratch_shapes=[
            pltpu.VMEM(transfer.shape, bf16),
            pltpu.VMEM((own, modes), f32),
            pltpu.VMEM((traps, patterns), i32),
            pltpu.VMEM((traps, patterns), i32),
            pltpu.VMEM((traps, patterns), f32),
            pltpu.VMEM((n_row, 2 * own, modes), bf16),
            pltpu.VMEM((CHUNKS, half) + block, f32),
            pltpu.VMEM((CHUNKS, half) + block, bf16),
            pltpu.VMEM((CHUNKS, half) + block, bf16),
            pltpu.VMEM((n_chip,) + block, bf16),
            pltpu.VMEM((n_chip,) + block, bf16),
            pltpu.VMEM((n_col,) + block, bf16),
            pltpu.VMEM((tile_rows, patterns), f32),
            pltpu.VMEM((tile_rows // 8, 8, patterns), f32),
            pltpu.VMEM((n_row, 2 * own, modes), bf16),
            pltpu.VMEM((n_row, 2 * own, modes), bf16),
            pltpu.VMEM((2 * own, modes), bf16),
            pltpu.VMEM((2 * own, modes), bf16),
            pltpu.VMEM((traps, patterns), f32),
            pltpu.VMEM((n_y, traps, patterns), bf16),
            pltpu.VMEM((2, traps, patterns), bf16),
            pltpu.VMEM((traps, patterns), bf16),
        ]
        + [
            dma((count,))
            for count in (5, n_row, n_row, CHUNKS, CHUNKS, n_chip, n_chip, n_chip, n_col, n_chip)
            + (n_row, n_row, n_y, n_y, 2, 2)
        ],
        compiler_params=pltpu.CompilerParams(
            collective_id=0, has_side_effects=True, vmem_limit_bytes=48 * 1024 * 1024
        ),
    )(*(pltpu.with_memory_space_constraint(array, pltpu.HBM) for array in arrays))
    return (far.reshape(pix_rows, 2, patterns), weights.T, slm.transpose(2, 0, 1))


def solution(mesh):
    placed = (P(None, "row", "col"), P("col", "row"), P(), P(), P())
    return jax.shard_map(
        body,
        mesh=mesh,
        in_specs=placed,
        out_specs=(P(("row", "col"), None, None), P(), P("col", None, "row")),
        check_vma=False,
    )
```

time: 57.7 us -> 47.3 us (0.82)
  Pallas kernels: 50.6 us -> 44.7 us
  local copies, waits for them, and re-layouts: 6.1 us -> 1.85 us
    pallas_call x1, Pallas kernels: 50.6 us -> 44.7 us  [body(): pl.pallas_call(functools.partial(kernel, n_row, n_col, (MODES / TRAPS) **...]
    unnamed x12 -> x2, local copies, waits for them, and re-layouts: 5.49 us -> 1.24 us
where the time goes in v2:
time: 47.3 us; the launch traced here: 47.2 us
  Pallas kernels  44.7 us (95%)
  local copies, waits for them, and re-layouts  1.85 us (4%)
  between operations  0.64 us (1%)
    pallas_call x1, Pallas kernels, body(): pl.pallas_call(functools.partial(kernel, n_row, n_col, (MODES / TRAPS) **...  44.7 us
    unnamed x2, local copies, waits for them, and re-layouts  1.24 us

profile of v2, /device:TPU:1, one launch (start us, length us, event | category | flops | bytes accessed | tf_op | source)
XLA Modules:
  0.0 47.2 jit_solution(2877046091442449794)
XLA Ops:
  0.6 44.7 %shard_map.76 = (bf16[16,256]{1,0:T(8,128)(2,1)S(1)}, f32[64,128]{1,0:T(8,128)S(1)}, f32[2,16,512]{2,1,0:T(8,128)S(1)}) custom-call(bf16[2,512,512]{2,1,0:T(8,128)(2,1)} %transfer_hbm.1, f32[16,512]{1,0:T(8,128)} %bitcast.8, s32[64,128]{1,0:T(8,128)} %bitcast.9, s32[64,128]{1,0:T(8,128)} %bitcast.10, f32[64,128]{1,0:T(8,128)} %bitcast.11), custom_call_target="tpu_custom_call" | custom-call | tf_op jit(solution)/shard_map/pallas_call | solution.py:474
  45.3 0.6 %reshape.9 = bf16[16,2,128]{2,1,0:T(2,128)(2,1)} reshape(bf16[16,256]{1,0:T(8,128)(2,1)S(1)} %get-tuple-element.6) | data formatting | bytes 16384 | tf_op jit(solution)/shard_map/reshape | solution.py:516
  45.9 0.6 %copy.10 = f32[128,64]{0,1:T(8,128)} copy(f32[128,64]{0,1:T(8,128)S(1)} %bitcast.7) | data formatting | bytes 65536
  46.5 0.6 %copy.11 = f32[512,2,16]{0,2,1:T(8,128)} copy(f32[512,2,16]{0,2,1:T(8,128)S(1)} %bitcast.6) | data formatting | bytes 131072
